TPU v7x, 256 devices: a whole 4x4x8 slice. The times are simulated.
256 devices in a mesh: req: 64 (over z, x, core), tp: 4 (over y).
Axes of the slice: x: 4, y: 4, z: 8, core: 2. Of those that a mesh axis runs over, the one named last changes fastest.
Arguments:
- patches: bfloat16 [65536, 1408], P('req')
- segment_ids: int32 [65536], P('req'), may hold values from 0 to 15, as said below
- grid_sides: int32 [65536], P('req'), may hold values from 8 to 32, as said below
- split_plan: int32 [64, 2], P('req'), may hold values from 0 to 960, as said below
- owner_dev: int32 [16384], P('req'), may hold values from 0 to 63, as said below
- dest_row: int32 [16384], P('req'), may hold values from 0 to 255, as said below
- ln_gain: float32 [1408], replicated, may hold values from 0.25 to 1.75
- ln_bias: float32 [1408], replicated, may hold values from -3 to 3
- w_qkv: bfloat16 [3, 1408, 1408], P(None, 'tp')
- w_out: bfloat16 [1408, 1408], P('tp'), may hold values from -0.625 to 0.625
- w_proj: bfloat16 [5632, 2048], P(None, 'tp'), may hold values from -0.078125 to 0.078125
Outputs:
- vision_tokens: bfloat16 [16384, 2048], P('req', 'tp')
Inputs may be any that keep to these rules, and one draw needn't show every extreme that they name: `segment_ids`: within each packed row the ids start at 0, never fall, and one id's patches are contiguous; an image with grid side s has s * s patches (the last image of the whole packing may be cut short) and lies in at most two neighbouring rows. `grid_sides`: all patches of one image share its grid side, a multiple of 8. split_plan[r, 0] is the number of patches of row r's first image that lie in row r - 1, split_plan[r, 1] the number of patches of row r's last image that lie in row r + 1; both are 0 where no image crosses. `owner_dev`: the merged tokens of one row form blocks of 8 consecutive merged tokens; each block goes whole to one owner, a row's blocks go to different owners, and every owner receives 1024 // 4 merged tokens. `dest_row`: every row of every owner's output receives exactly one merged token.
All inputs are finite; a program needn't handle non-finite values.
Results may differ from a plain program's by a relative error of at most 0.019.
Values may be sent and summed in bfloat16 or wider, within the bound.
No kernel may reach another device: no remote copies, remote signals or barrier semaphores. Data moves between devices by JAX's collectives and lax.ppermute only.
A program may use at most 128 MiB of HBM per device.

v0:
```python
import jax
import jax.numpy as jnp
from jax import lax
from jax.sharding import PartitionSpec as P

HD = 88


def extended(value, sides, width):
    for axis, dim in sides:
        count, length = (lax.axis_size(axis), value.shape[dim])
        up = [(i, (i + 1) % count) for i in range(count - 1)]
        down = [(j, i) for i, j in up]
        last = lax.slice_in_dim(value, length - width, length, axis=dim)
        leading = lax.slice_in_dim(value, 0, width, axis=dim)
        before = lax.ppermute(last, axis, up)
        after = lax.ppermute(leading, axis, down)
        value = jnp.concatenate([before, value, after], axis=dim)
    return value


def layer_norm(inputs, scale_vec, shift_vec):
    widened = inputs.astype(jnp.float32)
    centred = widened - jnp.mean(widened, axis=-1, keepdims=True)
    variance = jnp.mean(centred * centred, axis=-1, keepdims=True)
    return (centred * lax.rsqrt(variance + 1e-06) * scale_vec + shift_vec).astype(jnp.bfloat16)


def grid_positions(seg_row, side_row, first_offset):
    row_len = seg_row.shape[0]
    tok_index = jnp.arange(row_len, dtype=jnp.int32)
    boundary = jnp.concatenate([jnp.ones((1,), dtype=bool), seg_row[1:] != seg_row[:-1]])
    seg_start = lax.cummax(jnp.where(boundary, tok_index, 0), axis=0)
    offset = tok_index - seg_start + jnp.where(seg_row == 0, first_offset, 0)
    half_side = side_row // 2
    window = offset // 4
    corner = offset % 4
    return (2 * (window // half_side) + corner // 2, 2 * (window % half_side) + corner % 2)


def key_labels(seg_row, plan_row):
    row_len = seg_row.shape[0]
    tok_index = jnp.arange(row_len, dtype=jnp.int32)
    before = jnp.where(tok_index >= row_len - plan_row[0], 0, -1).astype(jnp.int32)
    after_keys = jnp.where(tok_index < plan_row[1], seg_row[row_len - 1], -1)
    return jnp.concatenate([before, seg_row, after_keys])


def rotate_pairs(channels, angles, axis_pos):
    quarter = channels.shape[axis_pos] // 2
    first_half = lax.slice_in_dim(channels, 0, quarter, axis=axis_pos)
    second_half = lax.slice_in_dim(channels, quarter, 2 * quarter, axis=axis_pos)
    cosine = jnp.cos(angles)
    sine_tab = jnp.sin(angles)
    return jnp.concatenate(
        [
            first_half * cosine - second_half * sine_tab,
            second_half * cosine + first_half * sine_tab,
        ],
        axis=axis_pos,
    )


def apply_rope(channels, row_angles, col_angles, axis_pos):
    half_width = channels.shape[axis_pos] // 2
    row_part = rotate_pairs(
        lax.slice_in_dim(channels, 0, half_width, axis=axis_pos), row_angles, axis_pos
    )
    col_part = rotate_pairs(
        lax.slice_in_dim(channels, half_width, 2 * half_width, axis=axis_pos), col_angles, axis_pos
    )
    return jnp.concatenate([row_part, col_part], axis=axis_pos)


def on_device(
    patches,
    segment_ids,
    grid_sides,
    split_plan,
    owner_dev,
    dest_row,
    ln_gain,
    ln_bias,
    w_qkv,
    w_out,
    w_proj,
):
    tok_count = patches.shape[0]
    feat_width = patches.shape[1]
    local_width = w_qkv.shape[1]
    local_heads = local_width // HD
    normed = layer_norm(patches, ln_gain, ln_bias)
    mixed_qkv = jnp.einsum("td,kcd->kct", normed, w_qkv, preferred_element_type=jnp.float32)
    grid_row, grid_col = grid_positions(segment_ids, grid_sides, split_plan[0, 0])
    quarter = HD // 4
    frequency = 10000.0 ** (-jnp.arange(quarter, dtype=jnp.float32) / quarter)
    row_angles = frequency[:, None] * grid_row.astype(jnp.float32)[None, :]
    col_angles = frequency[:, None] * grid_col.astype(jnp.float32)[None, :]
    shaped = mixed_qkv.reshape(3, local_heads, HD, tok_count)
    queries = apply_rope(shaped[0], row_angles, col_angles, 1).astype(jnp.bfloat16)
    key_rot = apply_rope(shaped[1], row_angles, col_angles, 1)
    key_value = jnp.stack([key_rot, shaped[2]]).astype(jnp.bfloat16)
    near_kv = extended(key_value, (("req", 3),), tok_count)
    near_keys = near_kv[0]
    near_values = near_kv[1]
    labels = key_labels(segment_ids, split_plan[0])
    block_rows = min(512, tok_count)
    w_heads = w_out.reshape(local_heads, HD, feat_width)

    def attend_block(first_row):
        q_block = lax.dynamic_slice_in_dim(queries, first_row, block_rows, 2)
        seg_block = lax.dynamic_slice_in_dim(segment_ids, first_row, block_rows, 0)
        allowed = seg_block[:, None] == labels[None, :]
        scores = jnp.einsum(
            "hcq,hck->hqk", q_block, near_keys, preferred_element_type=jnp.float32
        ) * HD ** (-0.5)
        scores = jnp.where(allowed[None], scores, -1e30)
        largest = jnp.max(scores, axis=-1, keepdims=True)
        weights = jnp.exp(scores - largest)
        attn_probs = (weights / jnp.sum(weights, axis=-1, keepdims=True)).astype(jnp.bfloat16)
        heads_out = jnp.einsum(
            "hqk,hck->hcq", attn_probs, near_values, preferred_element_type=jnp.float32
        ).astype(jnp.bfloat16)
        return jnp.einsum("hcq,hcd->qd", heads_out, w_heads, preferred_element_type=jnp.float32)

    block_starts = jnp.arange(tok_count // block_rows, dtype=jnp.int32) * block_rows
    partial_value = lax.map(attend_block, block_starts).reshape(tok_count, feat_width)
    attn_sum = lax.psum(partial_value.astype(jnp.bfloat16), "tp").astype(jnp.float32)
    mixed_rows = (patches.astype(jnp.float32) + attn_sum).astype(jnp.bfloat16)
    merged = mixed_rows.reshape(tok_count // 4, 4 * feat_width)
    projected = jnp.dot(merged, w_proj, preferred_element_type=jnp.float32).astype(jnp.bfloat16)
    per_owner = owner_dev.shape[0]
    peer_count = lax.axis_size("req")
    owner_slots = 2 * per_owner // peer_count
    matches = (owner_dev[:, None] == jnp.arange(peer_count, dtype=jnp.int32)[None, :]).astype(
        jnp.int32
    )
    arrival = jnp.sum(jnp.cumsum(matches, axis=0) * matches, axis=1) - 1
    send_slot = owner_dev * owner_slots + arrival
    out_cols = projected.shape[1]
    send_rows = (
        jnp.zeros((peer_count * owner_slots, out_cols), jnp.bfloat16).at[send_slot].set(projected)
    )
    send_dest = (
        jnp.full((peer_count * owner_slots,), per_owner, jnp.int32).at[send_slot].set(dest_row)
    )
    got_rows, got_dest = (
        lax.all_to_all(send_rows, "req", split_axis=0, concat_axis=0, tiled=True),
        lax.all_to_all(send_dest, "req", split_axis=0, concat_axis=0, tiled=True),
    )
    return jnp.zeros((per_owner, out_cols), jnp.bfloat16).at[got_dest].set(got_rows, mode="drop")


def solution(mesh):
    placed = (
        P("req", None),
        P("req"),
        P("req"),
        P("req", None),
        P("req"),
        P("req"),
        P(),
        P(),
        P(None, "tp", None),
        P("tp", None),
        P(None, "tp"),
    )
    return jax.shard_map(
        on_device, mesh=mesh, in_specs=placed, out_specs=P("req", "tp"), check_vma=False
    )
```

profile of v0, /device:TPU:1, one launch (start us, length us, event | category | flops | bytes accessed | tf_op | source)
XLA Modules:
  0.0 257.5 jit_solution(7537347584126004869)
XLA Ops:
  6.6 2.4 convert_reduce_fusion
  10.3 3.8 %fusion.38 = f32[3,352,1024]{2,1,0:T(8,128)S(1)} fusion(bf16[3,352,1408]{2,1,0:T(8,128)(2,1)S(1)} %copy-done, bf16[1024,1408]{1,0:T(8,128)(2,1)S(1)} %copy-done.2, f32[1408]{0:T(1024)S(1)} %copy-done.9, f32[1408]{0:T(1024)S(1)} %copy-done.10, f32[1024]{0:T(1024)S(1)} %add_rsqrt_fusion, f32[1024]{0:T(1024)S(1)} %broadcast_multiply_fusion), kind=kOutput, calls=%fused_computation.42 | convolution fusion | flops 3053715456 | bytes 10202112 | tf_op jit(solution)/shard_map/td,kcd->kct/dot_general | solution.py:93
  18.6 1.8 subtract_convert_fusion.1
  21.8 4.5 %collective-permute-start = (bf16[2,4,88,1024]{3,2,1,0:T(8,128)(2,1)}, bf16[2,4,88,1024]{3,2,1,0:T(8,128)(2,1)}, u32[]{:S(2)}, u32[]{:S(2)}) collective-permute-start(bf16[2,4,88,1024]{3,2,1,0:T(8,128)(2,1)} %pad_maximum_fusion.1), channel_id=1, source_target_pairs={{0,4},{4,8},{8,12},{12,16},{16,20},{20,24},{24,28},{28,32},{32,36}... | collective-permute-start | bytes 4325384 | tf_op jit(solution)/shard_map/ppermute | solution.py:16
  26.3 3.0 %collective-permute-start.1 = (bf16[2,4,88,1024]{3,2,1,0:T(8,128)(2,1)}, bf16[2,4,88,1024]{3,2,1,0:T(8,128)(2,1)}, u32[]{:S(2)}, u32[]{:S(2)}) collective-permute-start(bf16[2,4,88,1024]{3,2,1,0:T(8,128)(2,1)} %pad_maximum_fusion.1), channel_id=1, source_target_pairs={{4,0},{8,4},{12,8},{16,12},{20,16},{24,20},{28,24},{32,28},{36,32}... | collective-permute-start | bytes 4325384 | tf_op jit(solution)/shard_map/ppermute | solution.py:17
  33.2 9.4 %collective-permute-done = bf16[2,4,88,1024]{3,2,1,0:T(8,128)(2,1)} collective-permute-done((bf16[2,4,88,1024]{3,2,1,0:T(8,128)(2,1)}, bf16[2,4,88,1024]{3,2,1,0:T(8,128)(2,1)}, u32[]{:S(2)}, u32[]{:S(2)}) %collective-permute-start) | collective-permute-done | bytes 1441824 | tf_op jit(solution)/shard_map/ppermute | solution.py:16
  42.5 4.4 %collective-permute-done.1 = bf16[2,4,88,1024]{3,2,1,0:T(8,128)(2,1)} collective-permute-done((bf16[2,4,88,1024]{3,2,1,0:T(8,128)(2,1)}, bf16[2,4,88,1024]{3,2,1,0:T(8,128)(2,1)}, u32[]{:S(2)}, u32[]{:S(2)}) %collective-permute-start.1) | collective-permute-done | bytes 1441824 | tf_op jit(solution)/shard_map/ppermute | solution.py:17
  46.9 2.0 pad_maximum_fusion
  48.9 2.5 slice_bitcast_fusion
  51.4 69.2 %while.10 = (s32[]{:T(128)}, bf16[2,512,1408]{2,1,0:T(8,128)(2,1)}, s32[2]{0:T(128)S(1)}, s32[1024]{0:T(1024)S(1)}, s32[3072]{0:T(1024)S(1)}, /*index=5*/bf16[4,...) while((s32[]{:T(128)}, bf16[2,512,1408]{2,1,0:T(8,128)(2,1)}, ...), condition=%wide.region_11.12_spmd, body=%wide.region_8.11_spmd.sunk | while | flops 2761608192 | bytes 62073512 | solution.py:127
  55.1 15.8 %fusion.91 = (f32[4,512]{1,0:T(4,128)S(1)}, f32[4,512,3072]{2,1,0:T(8,128)}) fusion(pred[512,3072]{1,0:T(8,128)(4,1)S(1)} %broadcast_compare_fusion.2, bf16[4,88,3072]{2,1,0:T(8,128)(2,1)} %get-tuple-element.190, bf16[4,88,1024]{2,1,0:T(8,128)(2,1)S(1)} %get-tuple-element.189, s32[]{:T(128)S(6)} %select_n.147), kind=kOutput, calls=%fused_computation.129.clone.1 | convolution fusion | flops 1132465152 | bytes 29270020 | tf_op jit(solution)/shard_map/while/body/eval_jaxpr/sub | solution.py:119
  70.9 15.1 %fusion.92 = bf16[2,512,1408]{2,1,0:T(8,128)(2,1)} fusion(bf16[2,512,1408]{2,1,0:T(8,128)(2,1)} %get-tuple-element.173, s32[]{:T(128)} %get-tuple-element.172, bf16[4,88,1408]{2,1,0:T(8,128)(2,1)} %get-tuple-element.192, bf16[4,88,3072]{2,1,0:T(8,128)(2,1)} %get-tuple-element.191, f32[4,512,3072]{2,1,0:T(8,128)} %get-tuple-element.158, ...), kind=kOutput, calls=%fused_computation.13.clone.1 | convolution fusion | flops 1627570176 | bytes 31212032 | tf_op jit(solution)/shard_map/while/body/eval_jaxpr/hcq,hcd->qd/dot_general | solution.py:124
  89.8 15.8 %fusion.91 = (f32[4,512]{1,0:T(4,128)S(1)}, f32[4,512,3072]{2,1,0:T(8,128)}) fusion(pred[512,3072]{1,0:T(8,128)(4,1)S(1)} %broadcast_compare_fusion.2, bf16[4,88,3072]{2,1,0:T(8,128)(2,1)} %get-tuple-element.190, bf16[4,88,1024]{2,1,0:T(8,128)(2,1)S(1)} %get-tuple-element.189, s32[]{:T(128)S(6)} %select_n.147), kind=kOutput, calls=%fused_computation.129.clone.1 | convolution fusion | flops 1132465152 | bytes 29270020 | tf_op jit(solution)/shard_map/while/body/eval_jaxpr/sub | solution.py:119
  105.6 15.0 %fusion.92 = bf16[2,512,1408]{2,1,0:T(8,128)(2,1)} fusion(bf16[2,512,1408]{2,1,0:T(8,128)(2,1)} %get-tuple-element.173, s32[]{:T(128)} %get-tuple-element.172, bf16[4,88,1408]{2,1,0:T(8,128)(2,1)} %get-tuple-element.192, bf16[4,88,3072]{2,1,0:T(8,128)(2,1)} %get-tuple-element.191, f32[4,512,3072]{2,1,0:T(8,128)} %get-tuple-element.158, ...), kind=kOutput, calls=%fused_computation.13.clone.1 | convolution fusion | flops 1627570176 | bytes 31212032 | tf_op jit(solution)/shard_map/while/body/eval_jaxpr/hcq,hcd->qd/dot_general | solution.py:124
  122.2 1.6 scatter_custom_fusion
  124.5 13.9 %all-to-all-start = ((s32[64,8,1]{1,2,0:T(1,128)}), s32[64,8,1]{1,2,0:T(1,128)S(1)}, u32[]{:S(2)}, u32[]{:S(2)}) async-start(s32[64,8,1]{1,2,0:T(1,128)} %bitcast.6), calls=%async_computation | async-start | bytes 65536 | tf_op jit(solution)/shard_map/all_to_all | solution.py:149
  138.3 63.5 %all-reduce.2.cloned.1.call-done = bf16[1024,1408]{1,0:T(8,128)(2,1)} async-done(((bf16[1024,1408]{1,0:T(8,128)(2,1)}), bf16[1024,1408]{1,0:T(8,128)(2,1)}) %all-reduce.2.cloned.1.call-update) | async-done | bytes 2883600 | tf_op jit(solution)/shard_map/psum | solution.py:128
  201.9 4.1 %fusion.30 = bf16[1024,1408]{1,0:T(8,128)(2,1)} fusion(bf16[1024,1408]{1,0:T(8,128)(2,1)S(1)} %copy-done.3, bf16[1024,1408]{1,0:T(8,128)(2,1)} %all-reduce.2.cloned.1.call-done), kind=kLoop, calls=%fused_computation.34 | loop fusion | flops 5767168 | bytes 8650752 | tf_op jit(solution)/shard_map/convert_element_type | solution.py:129
  206.0 5.6 %reshape.244 = bf16[256,5632]{1,0:T(8,128)(2,1)} reshape(bf16[1024,1408]{1,0:T(8,128)(2,1)} %fusion.30) | data formatting | bytes 5767168 | tf_op jit(solution)/shard_map/reshape | solution.py:130
  211.6 5.3 %convolution_convert_fusion = bf16[256,512]{1,0:T(8,128)(2,1)S(1)} fusion(bf16[256,5632]{1,0:T(8,128)(2,1)} %reshape.244, bf16[5632,512]{1,0:T(8,128)(2,1)} %param.23), kind=kOutput, calls=%fused_computation.47 | convolution fusion | flops 1476526080 | bytes 8912896 | tf_op jit(solution)/shard_map/dot_general | solution.py:131
  216.9 2.3 scatter_custom_fusion.1
  219.3 10.7 %all-to-all-start.1 = ((bf16[64,8,512]{2,1,0:T(8,128)(2,1)}), bf16[64,8,512]{2,1,0:T(8,128)(2,1)S(1)}, u32[]{:S(2)}, u32[]{:S(2)}) async-start(bf16[64,8,512]{2,1,0:T(8,128)(2,1)} %bitcast.23), calls=%async_computation.1 | async-start | bytes 1048576 | tf_op jit(solution)/shard_map/all_to_all | solution.py:148
  232.8 14.9 %all-to-all-done.1 = bf16[64,8,512]{2,1,0:T(8,128)(2,1)S(1)} async-done(((bf16[64,8,512]{2,1,0:T(8,128)(2,1)}), bf16[64,8,512]{2,1,0:T(8,128)(2,1)S(1)}, u32[]{:S(2)}, u32[]{:S(2)}) %all-to-all-start.1) | async-done | bytes 524320 | tf_op jit(solution)/shard_map/all_to_all | solution.py:148
  247.6 3.0 %scatter_custom_fusion.2 = bf16[256,512]{1,0:T(8,128)(2,1)} fusion(s32[512]{0:T(512)S(1)} %bitcast.91, bf16[64,8,512]{2,1,0:T(8,128)(2,1)S(1)} %all-to-all-done.1, bf16[]{:T(256)} %constant.105.clone.1), kind=kCustom, calls=%fused_computation.50 | custom fusion | bytes 786434 | tf_op jit(solution)/shard_map/scatter | solution.py:151
  (67 shorter events, 18.8 us)
Async XLA Ops:
  6.5 3.7 %copy-start = (bf16[3,352,1408]{2,1,0:T(8,128)(2,1)S(1)}, bf16[3,352,1408]{2,1,0:T(8,128)(2,1)}, u32[]{:S(2)}) copy-start(bf16[3,352,1408]{2,1,0:T(8,128)(2,1)} %param.21) | copy-start | bytes 8921092
  6.5 195.3 %all-reduce.2.cloned.1.call-start = ((), (), s32[]{:S(2)}) async-start(), calls=%async_computation.2 | async-start | bytes 5767168 | tf_op jit(solution)/shard_map/psum | solution.py:128
  6.5 2.8 %copy-start.2 = (bf16[1024,1408]{1,0:T(8,128)(2,1)S(1)}, bf16[1024,1408]{1,0:T(8,128)(2,1)}, u32[]{:S(2)}) copy-start(bf16[1024,1408]{1,0:T(8,128)(2,1)} %param.13) | copy-start | bytes 8650756
  6.6 3.7 %copy-start.9 = (f32[1408]{0:T(1024)S(1)}, f32[1408]{0:T(1024)}, u32[]{:S(2)}) copy-start(f32[1408]{0:T(1024)} %param.20) | copy-start | bytes 16900
  6.6 3.7 %copy-start.10 = (f32[1408]{0:T(1024)S(1)}, f32[1408]{0:T(1024)}, u32[]{:S(2)}) copy-start(f32[1408]{0:T(1024)} %param.19) | copy-start | bytes 16900
  14.1 1.5 copy-start.8
  14.1 2.1 copy-start.5
  14.1 2.8 %copy-start.7 = (s32[1024]{0:T(1024)S(1)}, s32[1024]{0:T(1024)}, u32[]{:S(2)}) copy-start(s32[1024]{0:T(1024)} %param.15) | copy-start | bytes 12292
  21.8 20.8 %collective-permute-start = (bf16[2,4,88,1024]{3,2,1,0:T(8,128)(2,1)}, bf16[2,4,88,1024]{3,2,1,0:T(8,128)(2,1)}, u32[]{:S(2)}, u32[]{:S(2)}) collective-permute-start(bf16[2,4,88,1024]{3,2,1,0:T(8,128)(2,1)} %pad_maximum_fusion.1), channel_id=1, source_target_pairs={{0,4},{4,8},{8,12},{12,16},{16,20},{20,24},{24,28},{28,32},{32,36}... | collective-permute-start | bytes 4325384 | tf_op jit(solution)/shard_map/ppermute | solution.py:16
  26.3 20.6 %collective-permute-start.1 = (bf16[2,4,88,1024]{3,2,1,0:T(8,128)(2,1)}, bf16[2,4,88,1024]{3,2,1,0:T(8,128)(2,1)}, u32[]{:S(2)}, u32[]{:S(2)}) collective-permute-start(bf16[2,4,88,1024]{3,2,1,0:T(8,128)(2,1)} %pad_maximum_fusion.1), channel_id=1, source_target_pairs={{4,0},{8,4},{12,8},{16,12},{20,16},{24,20},{28,24},{32,28},{36,32}... | collective-permute-start | bytes 4325384 | tf_op jit(solution)/shard_map/ppermute | solution.py:17
  48.9 2.5 copy-start.4
  120.5 0.7 copy-start.6
  120.6 81.3 %copy-start.3 = (bf16[1024,1408]{1,0:T(8,128)(2,1)S(1)}, bf16[1024,1408]{1,0:T(8,128)(2,1)}, u32[]{:S(2)}) copy-start(bf16[1024,1408]{1,0:T(8,128)(2,1)} %param.13) | copy-start | bytes 8650756
  124.5 94.8 %all-to-all-start = ((s32[64,8,1]{1,2,0:T(1,128)}), s32[64,8,1]{1,2,0:T(1,128)S(1)}, u32[]{:S(2)}, u32[]{:S(2)}) async-start(s32[64,8,1]{1,2,0:T(1,128)} %bitcast.6), calls=%async_computation | async-start | bytes 65536 | tf_op jit(solution)/shard_map/all_to_all | solution.py:149
  211.6 39.0 %copy-start.1 = (bf16[3,352,1408]{2,1,0:T(8,128)(2,1)S(1)}, bf16[3,352,1408]{2,1,0:T(8,128)(2,1)}, u32[]{:S(2)}) copy-start(bf16[3,352,1408]{2,1,0:T(8,128)(2,1)} %param.21) | copy-start | bytes 8921092
  219.3 28.4 %all-to-all-start.1 = ((bf16[64,8,512]{2,1,0:T(8,128)(2,1)}), bf16[64,8,512]{2,1,0:T(8,128)(2,1)S(1)}, u32[]{:S(2)}, u32[]{:S(2)}) async-start(bf16[64,8,512]{2,1,0:T(8,128)(2,1)} %bitcast.23), calls=%async_computation.1 | async-start | bytes 1048576 | tf_op jit(solution)/shard_map/all_to_all | solution.py:148
Sparse Core Ops, SparseCore 0:
  120.7 81.1 all-reduce.1
where the time goes:
time: 258 us
  waiting for transfers between devices  92.2 us (36%)
  matrix products  70.8 us (27%)
  starting transfers between devices  32 us (12%)
  local copies, waits for them, and re-layouts  22.7 us (9%)
  other arithmetic  21.3 us (8%)
  between operations  14.3 us (6%)
  loops' own time  4.17 us (2%)
    psum x1, waiting for transfers between devices, on_device(): lax.psum(partial_value.astype(jnp.bfloat16), 'tp').astype(jnp.float32)  63.5 us
    sub x2, matrix products, attend_block(): weights = jnp.exp(scores - largest)  31.7 us
    dot_general x2, matrix products, attend_block(): jnp.einsum('hcq,hcd->qd', heads_out, w_heads, preferred_element_type=jnp....  30.1 us
    all_to_all x1, waiting for transfers between devices, on_device(): lax.all_to_all(send_rows, 'req', split_axis=0, concat_axis=0, tiled=True)  14.9 us
    all_to_all x1, starting transfers between devices, on_device(): lax.all_to_all(send_dest, 'req', split_axis=0, concat_axis=0, tiled=True)  13.9 us
    all_to_all x1, starting transfers between devices, on_device(): lax.all_to_all(send_rows, 'req', split_axis=0, concat_axis=0, tiled=True)  10.7 us
    ppermute x1, waiting for transfers between devices, extended(): before = lax.ppermute(last, axis, up)  9.36 us
    reshape x1, local copies, waits for them, and re-layouts, on_device(): merged = mixed_rows.reshape(tok_count // 4, 4 * feat_width)  5.62 us
  transfers between devices with their start and end apart: 5, of which 4 were waited for; matrix products, arithmetic and copies ran while one was open for 10% of the time, Pallas kernels for 0%

commit v1 on v0

--- a/solution.py
+++ b/solution.py
@@ -125,7 +125,9 @@
 
     block_starts = jnp.arange(tok_count // block_rows, dtype=jnp.int32) * block_rows
     partial_value = lax.map(attend_block, block_starts).reshape(tok_count, feat_width)
-    attn_sum = lax.psum(partial_value.astype(jnp.bfloat16), "tp").astype(jnp.float32)
+    attn_sum = jnp.sum(lax.all_gather(partial_value.astype(jnp.bfloat16), "tp"), axis=0).astype(
+        jnp.float32
+    )
     mixed_rows = (patches.astype(jnp.float32) + attn_sum).astype(jnp.bfloat16)
     merged = mixed_rows.reshape(tok_count // 4, 4 * feat_width)
     projected = jnp.dot(merged, w_proj, preferred_element_type=jnp.float32).astype(jnp.bfloat16)

time: 258 us -> 302 us (1.17)
  waiting for transfers between devices: 92.2 us -> 129 us
  other arithmetic: 21.3 us -> 28.9 us
    all_gather x0 -> x1, waiting for transfers between devices: none -> 99.2 us  [on_device(): lax.all_gather(partial_value.astype(jnp.bfloat16), 'tp')]
    psum x1 -> x0, waiting for transfers between devices: 63.5 us -> none  [on_device(): lax.psum(partial_value.astype(jnp.bfloat16), 'tp').astype(jnp.float32)]
    reduce_sum x0 -> x1, other arithmetic: none -> 8.43 us  [on_device(): jnp.sum(lax.all_gather(partial_value.astype(jnp.bfloat16), 'tp'), axis=0)]
  transfers between devices with their start and end apart: 5 -> 5, of which waited for: 4 -> 4; matrix products, arithmetic and copies ran while one was open for 10% -> 11% of each run, Pallas kernels for 0% -> 0%
where the time goes in v1:
time: 302 us
  waiting for transfers between devices  129 us (43%)
  matrix products  70.8 us (23%)
  starting transfers between devices  32 us (11%)
  other arithmetic  28.9 us (10%)
  local copies, waits for them, and re-layouts  22.7 us (8%)
  between operations  14.3 us (5%)
  loops' own time  4.17 us (1%)
    all_gather x1, waiting for transfers between devices, on_device(): lax.all_gather(partial_value.astype(jnp.bfloat16), 'tp')  99.2 us
    sub x2, matrix products, attend_block(): weights = jnp.exp(scores - largest)  31.7 us
    dot_general x2, matrix products, attend_block(): jnp.einsum('hcq,hcd->qd', heads_out, w_heads, preferred_element_type=jnp....  30.1 us
    all_to_all x1, waiting for transfers between devices, on_device(): lax.all_to_all(send_rows, 'req', split_axis=0, concat_axis=0, tiled=True)  14.9 us
    all_to_all x1, starting transfers between devices, on_device(): lax.all_to_all(send_dest, 'req', split_axis=0, concat_axis=0, tiled=True)  13.9 us
    all_to_all x1, starting transfers between devices, on_device(): lax.all_to_all(send_rows, 'req', split_axis=0, concat_axis=0, tiled=True)  10.7 us
    ppermute x1, waiting for transfers between devices, extended(): before = lax.ppermute(last, axis, up)  10.2 us
    reduce_sum x1, other arithmetic, on_device(): jnp.sum(lax.all_gather(partial_value.astype(jnp.bfloat16), 'tp'), axis=0)  8.43 us
  transfers between devices with their start and end apart: 5, of which 4 were waited for; matrix products, arithmetic and copies ran while one was open for 11% of the time, Pallas kernels for 0%

profile of v1, /device:TPU:1, one launch (start us, length us, event | category | flops | bytes accessed | tf_op | source)
XLA Modules:
  0.0 301.7 jit_solution(14051829650097646454)
XLA Ops:
  6.6 2.4 convert_reduce_fusion
  10.3 3.8 %fusion.38 = f32[3,352,1024]{2,1,0:T(8,128)S(1)} fusion(bf16[3,352,1408]{2,1,0:T(8,128)(2,1)S(1)} %copy-done, bf16[1024,1408]{1,0:T(8,128)(2,1)S(1)} %copy-done.2, f32[1408]{0:T(1024)S(1)} %copy-done.8, f32[1408]{0:T(1024)S(1)} %copy-done.9, f32[1024]{0:T(1024)S(1)} %add_rsqrt_fusion, f32[1024]{0:T(1024)S(1)} %broadcast_multiply_fusion), kind=kOutput, calls=%fused_computation.42 | convolution fusion | flops 3053715456 | bytes 10202112 | tf_op jit(solution)/shard_map/td,kcd->kct/dot_general | solution.py:93
  18.6 1.8 subtract_convert_fusion.1
  21.8 4.5 %collective-permute-start = (bf16[2,4,88,1024]{3,2,1,0:T(8,128)(2,1)}, bf16[2,4,88,1024]{3,2,1,0:T(8,128)(2,1)}, u32[]{:S(2)}, u32[]{:S(2)}) collective-permute-start(bf16[2,4,88,1024]{3,2,1,0:T(8,128)(2,1)} %pad_maximum_fusion.1), channel_id=1, source_target_pairs={{0,4},{4,8},{8,12},{12,16},{16,20},{20,24},{24,28},{28,32},{32,36}... | collective-permute-start | bytes 4325384 | tf_op jit(solution)/shard_map/ppermute | solution.py:16
  26.3 3.0 %collective-permute-start.1 = (bf16[2,4,88,1024]{3,2,1,0:T(8,128)(2,1)}, bf16[2,4,88,1024]{3,2,1,0:T(8,128)(2,1)}, u32[]{:S(2)}, u32[]{:S(2)}) collective-permute-start(bf16[2,4,88,1024]{3,2,1,0:T(8,128)(2,1)} %pad_maximum_fusion.1), channel_id=1, source_target_pairs={{4,0},{8,4},{12,8},{16,12},{20,16},{24,20},{28,24},{32,28},{36,32}... | collective-permute-start | bytes 4325384 | tf_op jit(solution)/shard_map/ppermute | solution.py:17
  32.3 10.2 %collective-permute-done = bf16[2,4,88,1024]{3,2,1,0:T(8,128)(2,1)} collective-permute-done((bf16[2,4,88,1024]{3,2,1,0:T(8,128)(2,1)}, bf16[2,4,88,1024]{3,2,1,0:T(8,128)(2,1)}, u32[]{:S(2)}, u32[]{:S(2)}) %collective-permute-start) | collective-permute-done | bytes 1441824 | tf_op jit(solution)/shard_map/ppermute | solution.py:16
  42.5 4.4 %collective-permute-done.1 = bf16[2,4,88,1024]{3,2,1,0:T(8,128)(2,1)} collective-permute-done((bf16[2,4,88,1024]{3,2,1,0:T(8,128)(2,1)}, bf16[2,4,88,1024]{3,2,1,0:T(8,128)(2,1)}, u32[]{:S(2)}, u32[]{:S(2)}) %collective-permute-start.1) | collective-permute-done | bytes 1441824 | tf_op jit(solution)/shard_map/ppermute | solution.py:17
  46.9 2.0 pad_maximum_fusion
  48.9 2.5 slice_bitcast_fusion
  51.3 69.2 %while.10 = (s32[]{:T(128)}, bf16[2,512,1408]{2,1,0:T(8,128)(2,1)}, s32[2]{0:T(128)S(1)}, s32[1024]{0:T(1024)S(1)}, s32[3072]{0:T(1024)S(1)}, /*index=5*/bf16[4,...) while((s32[]{:T(128)}, bf16[2,512,1408]{2,1,0:T(8,128)(2,1)}, ...), condition=%wide.region_11.12_spmd, body=%wide.region_8.11_spmd.sunk | while | flops 2761608192 | bytes 62073512 | solution.py:127
  55.1 15.8 %fusion.91 = (f32[4,512]{1,0:T(4,128)S(1)}, f32[4,512,3072]{2,1,0:T(8,128)}) fusion(pred[512,3072]{1,0:T(8,128)(4,1)S(1)} %broadcast_compare_fusion.2, bf16[4,88,3072]{2,1,0:T(8,128)(2,1)} %get-tuple-element.190, bf16[4,88,1024]{2,1,0:T(8,128)(2,1)S(1)} %get-tuple-element.189, s32[]{:T(128)S(6)} %select_n.147), kind=kOutput, calls=%fused_computation.129.clone.1 | convolution fusion | flops 1132465152 | bytes 29270020 | tf_op jit(solution)/shard_map/while/body/eval_jaxpr/sub | solution.py:119
  70.9 15.1 %fusion.92 = bf16[2,512,1408]{2,1,0:T(8,128)(2,1)} fusion(bf16[2,512,1408]{2,1,0:T(8,128)(2,1)} %get-tuple-element.173, s32[]{:T(128)} %get-tuple-element.172, bf16[4,88,1408]{2,1,0:T(8,128)(2,1)} %get-tuple-element.192, bf16[4,88,3072]{2,1,0:T(8,128)(2,1)} %get-tuple-element.191, f32[4,512,3072]{2,1,0:T(8,128)} %get-tuple-element.158, ...), kind=kOutput, calls=%fused_computation.13.clone.1 | convolution fusion | flops 1627570176 | bytes 31212032 | tf_op jit(solution)/shard_map/while/body/eval_jaxpr/hcq,hcd->qd/dot_general | solution.py:124
  89.7 15.8 %fusion.91 = (f32[4,512]{1,0:T(4,128)S(1)}, f32[4,512,3072]{2,1,0:T(8,128)}) fusion(pred[512,3072]{1,0:T(8,128)(4,1)S(1)} %broadcast_compare_fusion.2, bf16[4,88,3072]{2,1,0:T(8,128)(2,1)} %get-tuple-element.190, bf16[4,88,1024]{2,1,0:T(8,128)(2,1)S(1)} %get-tuple-element.189, s32[]{:T(128)S(6)} %select_n.147), kind=kOutput, calls=%fused_computation.129.clone.1 | convolution fusion | flops 1132465152 | bytes 29270020 | tf_op jit(solution)/shard_map/while/body/eval_jaxpr/sub | solution.py:119
  105.6 15.0 %fusion.92 = bf16[2,512,1408]{2,1,0:T(8,128)(2,1)} fusion(bf16[2,512,1408]{2,1,0:T(8,128)(2,1)} %get-tuple-element.173, s32[]{:T(128)} %get-tuple-element.172, bf16[4,88,1408]{2,1,0:T(8,128)(2,1)} %get-tuple-element.192, bf16[4,88,3072]{2,1,0:T(8,128)(2,1)} %get-tuple-element.191, f32[4,512,3072]{2,1,0:T(8,128)} %get-tuple-element.158, ...), kind=kOutput, calls=%fused_computation.13.clone.1 | convolution fusion | flops 1627570176 | bytes 31212032 | tf_op jit(solution)/shard_map/while/body/eval_jaxpr/hcq,hcd->qd/dot_general | solution.py:124
  124.5 13.9 %all-to-all-start = ((s32[64,8,1]{1,2,0:T(1,128)}), s32[64,8,1]{1,2,0:T(1,128)S(1)}, u32[]{:S(2)}, u32[]{:S(2)}) async-start(s32[64,8,1]{1,2,0:T(1,128)} %bitcast.6), calls=%async_computation | async-start | bytes 65536 | tf_op jit(solution)/shard_map/all_to_all | solution.py:151
  138.4 99.2 %all-gather.2.cloned.1.call-done = bf16[4,1024,1408]{2,1,0:T(8,128)(2,1)} async-done(((bf16[1,1024,1408]{2,1,0:T(8,128)(2,1)}), bf16[4,1024,1408]{2,1,0:T(8,128)(2,1)}) %all-gather.2.cloned.1.call-update) | async-done | bytes 11534352 | tf_op jit(solution)/shard_map/all_gather | solution.py:128
  237.5 8.4 %reduce_sum.51 = bf16[1024,1408]{1,0:T(8,128)(2,1)} reduce(bf16[4,1024,1408]{2,1,0:T(8,128)(2,1)} %all-gather.2.cloned.1.call-done, bf16[]{:T(256)} %constant.106.clone.1), dimensions={0}, to_apply=%region_12.13 | reduce | flops 4325376 | bytes 14417922 | tf_op jit(solution)/shard_map/reduce_sum | solution.py:128
  246.0 4.2 %fusion.30 = bf16[1024,1408]{1,0:T(8,128)(2,1)} fusion(bf16[1024,1408]{1,0:T(8,128)(2,1)S(1)} %copy-done.3, bf16[1024,1408]{1,0:T(8,128)(2,1)} %reduce_sum.51), kind=kLoop, calls=%fused_computation.34 | loop fusion | flops 5767168 | bytes 8650752 | tf_op jit(solution)/shard_map/convert_element_type | solution.py:131
  250.2 5.6 %reshape.254 = bf16[256,5632]{1,0:T(8,128)(2,1)} reshape(bf16[1024,1408]{1,0:T(8,128)(2,1)} %fusion.30) | data formatting | bytes 5767168 | tf_op jit(solution)/shard_map/reshape | solution.py:132
  255.8 5.3 %convolution_convert_fusion = bf16[256,512]{1,0:T(8,128)(2,1)S(1)} fusion(bf16[256,5632]{1,0:T(8,128)(2,1)} %reshape.254, bf16[5632,512]{1,0:T(8,128)(2,1)} %param.23), kind=kOutput, calls=%fused_computation.47 | convolution fusion | flops 1476526080 | bytes 8912896 | tf_op jit(solution)/shard_map/dot_general | solution.py:133
  261.1 2.3 scatter_custom_fusion.1
  263.4 10.7 %all-to-all-start.1 = ((bf16[64,8,512]{2,1,0:T(8,128)(2,1)}), bf16[64,8,512]{2,1,0:T(8,128)(2,1)S(1)}, u32[]{:S(2)}, u32[]{:S(2)}) async-start(bf16[64,8,512]{2,1,0:T(8,128)(2,1)} %bitcast.23), calls=%async_computation.1 | async-start | bytes 1048576 | tf_op jit(solution)/shard_map/all_to_all | solution.py:150
  276.9 14.9 %all-to-all-done.1 = bf16[64,8,512]{2,1,0:T(8,128)(2,1)S(1)} async-done(((bf16[64,8,512]{2,1,0:T(8,128)(2,1)}), bf16[64,8,512]{2,1,0:T(8,128)(2,1)S(1)}, u32[]{:S(2)}, u32[]{:S(2)}) %all-to-all-start.1) | async-done | bytes 524320 | tf_op jit(solution)/shard_map/all_to_all | solution.py:150
  291.8 3.0 %scatter_custom_fusion.2 = bf16[256,512]{1,0:T(8,128)(2,1)} fusion(s32[512]{0:T(512)S(1)} %bitcast.91, bf16[64,8,512]{2,1,0:T(8,128)(2,1)S(1)} %all-to-all-done.1, bf16[]{:T(256)} %constant.106.clone.1), kind=kCustom, calls=%fused_computation.50 | custom fusion | bytes 786434 | tf_op jit(solution)/shard_map/scatter | solution.py:153
  (66 shorter events, 19.5 us)
Async XLA Ops:
  6.5 3.7 %copy-start = (bf16[3,352,1408]{2,1,0:T(8,128)(2,1)S(1)}, bf16[3,352,1408]{2,1,0:T(8,128)(2,1)}, u32[]{:S(2)}) copy-start(bf16[3,352,1408]{2,1,0:T(8,128)(2,1)} %param.21) | copy-start | bytes 8921092
  6.5 231.0 %all-gather.2.cloned.1.call-start = ((), (), s32[]{:S(2)}) async-start(), calls=%async_computation.2 | async-start | bytes 14417920 | tf_op jit(solution)/shard_map/all_gather | solution.py:128
  6.5 2.8 copy-start.2
  6.6 3.7 %copy-start.8 = (f32[1408]{0:T(1024)S(1)}, f32[1408]{0:T(1024)}, u32[]{:S(2)}) copy-start(f32[1408]{0:T(1024)} %param.20) | copy-start | bytes 16900
  6.6 3.7 %copy-start.9 = (f32[1408]{0:T(1024)S(1)}, f32[1408]{0:T(1024)}, u32[]{:S(2)}) copy-start(f32[1408]{0:T(1024)} %param.19) | copy-start | bytes 16900
  14.1 1.5 copy-start.7
  14.1 2.1 copy-start.4
  14.1 2.8 copy-start.6
  21.8 20.8 %collective-permute-start = (bf16[2,4,88,1024]{3,2,1,0:T(8,128)(2,1)}, bf16[2,4,88,1024]{3,2,1,0:T(8,128)(2,1)}, u32[]{:S(2)}, u32[]{:S(2)}) collective-permute-start(bf16[2,4,88,1024]{3,2,1,0:T(8,128)(2,1)} %pad_maximum_fusion.1), channel_id=1, source_target_pairs={{0,4},{4,8},{8,12},{12,16},{16,20},{20,24},{24,28},{28,32},{32,36}... | collective-permute-start | bytes 4325384 | tf_op jit(solution)/shard_map/ppermute | solution.py:16
  26.3 20.6 %collective-permute-start.1 = (bf16[2,4,88,1024]{3,2,1,0:T(8,128)(2,1)}, bf16[2,4,88,1024]{3,2,1,0:T(8,128)(2,1)}, u32[]{:S(2)}, u32[]{:S(2)}) collective-permute-start(bf16[2,4,88,1024]{3,2,1,0:T(8,128)(2,1)} %pad_maximum_fusion.1), channel_id=1, source_target_pairs={{4,0},{8,4},{12,8},{16,12},{20,16},{24,20},{28,24},{32,28},{36,32}... | collective-permute-start | bytes 4325384 | tf_op jit(solution)/shard_map/ppermute | solution.py:17
  120.6 0.7 copy-start.5
  124.5 138.9 %all-to-all-start = ((s32[64,8,1]{1,2,0:T(1,128)}), s32[64,8,1]{1,2,0:T(1,128)S(1)}, u32[]{:S(2)}, u32[]{:S(2)}) async-start(s32[64,8,1]{1,2,0:T(1,128)} %bitcast.6), calls=%async_computation | async-start | bytes 65536 | tf_op jit(solution)/shard_map/all_to_all | solution.py:151
  138.3 107.6 %copy-start.3 = (bf16[1024,1408]{1,0:T(8,128)(2,1)S(1)}, bf16[1024,1408]{1,0:T(8,128)(2,1)}, u32[]{:S(2)}) copy-start(bf16[1024,1408]{1,0:T(8,128)(2,1)} %param.13) | copy-start | bytes 8650756
  255.8 39.0 %copy-start.1 = (bf16[3,352,1408]{2,1,0:T(8,128)(2,1)S(1)}, bf16[3,352,1408]{2,1,0:T(8,128)(2,1)}, u32[]{:S(2)}) copy-start(bf16[3,352,1408]{2,1,0:T(8,128)(2,1)} %param.21) | copy-start | bytes 8921092
  263.4 28.4 %all-to-all-start.1 = ((bf16[64,8,512]{2,1,0:T(8,128)(2,1)}), bf16[64,8,512]{2,1,0:T(8,128)(2,1)S(1)}, u32[]{:S(2)}, u32[]{:S(2)}) async-start(bf16[64,8,512]{2,1,0:T(8,128)(2,1)} %bitcast.23), calls=%async_computation.1 | async-start | bytes 1048576 | tf_op jit(solution)/shard_map/all_to_all | solution.py:150
Sparse Core Ops, SparseCore 0:
  120.7 116.7 all-gather.1
